TPU v7x, 32 devices: a whole 2x2x4 slice. The times are simulated.
32 devices in a mesh: segment: 4 (over z), seq: 4 (over y, core), dp: 2 (over x).
Axes of the slice: x: 2, y: 2, z: 4, core: 2. Of those that a mesh axis runs over, the one named last changes fastest.
Arguments:
- clean: bfloat16 [2, 512, 64], P('dp', 'seq'), may hold values from -16 to 16
- noise: bfloat16 [2, 512, 128], P('dp', 'seq'), may hold values from -24 to 24
- timesteps: int32 [2, 2], replicated, may hold values from 20 to 979
- text_vec: float32 [2, 256], P('dp'), may hold values from -6 to 6
- w_embed: bfloat16 [4, 64, 3072], P('segment'), may hold values from -0.75 to 0.75
- w_time: bfloat16 [4, 256, 3072], P('segment'), may hold values from -0.375 to 0.375
- w_mod: bfloat16 [4, 3072, 15360], P('segment', None, 'seq'), may hold values from -0.109375 to 0.109375
- w_qkv: bfloat16 [4, 3072, 4, 3, 128], P('segment', None, 'seq'), may hold values from -0.109375 to 0.109375
- w_out: bfloat16 [4, 4, 128, 3072], P('segment', 'seq'), may hold values from -0.25 to 0.25
- qk_gain: float32 [4, 2, 128], P('segment'), may hold values from 1.5 to 2.5
- w_final: bfloat16 [4, 3072, 64], P('segment'), may hold values from -0.109375 to 0.109375
Outputs:
- sample_grad: float32 [2, 512, 64], P('dp', 'seq')
- final_grads: float32 [4, 3072, 64], P('segment')
All inputs are finite; a program needn't handle non-finite values. Where the computation divides by a largest or mean magnitude, that divisor is 1e-20 or more.
Results may differ from a plain program's by a relative error of at most 0.025.
Values may be sent and summed in bfloat16 or wider, within the bound.
No kernel may reach another device: no remote copies, remote signals or barrier semaphores. Data moves between devices by JAX's collectives and lax.ppermute only.
A program may use at most 192 MiB of HBM per device.

v0:
```python
import math
import jax
import jax.numpy as jnp
from jax import lax
from jax.sharding import PartitionSpec as P

SHIFT = 7.0
EPS = 1e-06
ADV_WEIGHT = 3.0


def from_root(value, axis, source):
    kept = jnp.where(lax.axis_index(axis) == source, value, 0).astype(value.dtype)
    return lax.psum(kept, axis)


def noise_level(step):
    fraction = step.astype(jnp.float32) / 1000.0
    return SHIFT * fraction / (1.0 + (SHIFT - 1.0) * fraction)


def time_features(step, feature_count):
    half_width = feature_count // 2
    frequency = jnp.exp(-math.log(10000.0) * jnp.arange(half_width, dtype=jnp.float32) / half_width)
    angles = step.astype(jnp.float32) * frequency
    return jnp.concatenate([jnp.cos(angles), jnp.sin(angles)])


def condition(step, text_row, time_w, mod_w):
    features = (time_features(step, text_row.shape[0]) + text_row).astype(jnp.bfloat16)
    hidden = jax.nn.silu(jnp.dot(features, time_w, preferred_element_type=jnp.float32)).astype(
        jnp.bfloat16
    )
    return jnp.dot(hidden, mod_w, preferred_element_type=jnp.float32)


def normalize(values):
    row_mean = jnp.mean(values, axis=-1, keepdims=True)
    centered = values - row_mean
    inverse = lax.rsqrt(jnp.mean(centered * centered, axis=-1, keepdims=True) + EPS)
    return (centered * inverse, inverse)


def normalize_back(gradient, normed, inverse):
    return inverse * (
        gradient
        - jnp.mean(gradient, axis=-1, keepdims=True)
        - normed * jnp.mean(gradient * normed, axis=-1, keepdims=True)
    )


def rms_scale(values, gain_vec):
    inverse = lax.rsqrt(jnp.mean(values * values, axis=-1, keepdims=True) + EPS)
    unit_vec = values * inverse
    return (unit_vec * gain_vec, unit_vec, inverse)


def rms_back(gradient, unit_vec, inverse, gain_vec):
    scaled = gradient * gain_vec
    return inverse * (scaled - unit_vec * jnp.mean(scaled * unit_vec, axis=-1, keepdims=True))


def head_front(normed_in, head_w, gains):
    head_width = head_w.shape[-1]
    flat_w = head_w.reshape(head_w.shape[0], 3 * head_width)
    projected = jnp.dot(normed_in, flat_w, preferred_element_type=jnp.float32)
    queries, q_unit, q_inverse = rms_scale(projected[:, :head_width], gains[0])
    key_vecs, k_unit, k_inverse = rms_scale(projected[:, head_width : 2 * head_width], gains[1])
    query_b = queries.astype(jnp.bfloat16)
    key_b = key_vecs.astype(jnp.bfloat16)
    value_b = projected[:, 2 * head_width :].astype(jnp.bfloat16)
    scores = jnp.dot(query_b, key_b.T, preferred_element_type=jnp.float32) / math.sqrt(head_width)
    weights = jnp.exp(scores)
    soft_max = weights / jnp.sum(weights, axis=-1, keepdims=True)
    head_out = jnp.dot(
        soft_max.astype(jnp.bfloat16), value_b, preferred_element_type=jnp.float32
    ).astype(jnp.bfloat16)
    return (head_out, (q_unit, q_inverse, k_unit, k_inverse, query_b, key_b, value_b, soft_max))


def head_back(grad_out, stored, gains):
    q_unit, q_inverse, k_unit, k_inverse, query_b, key_b, value_b, soft_max = stored
    head_width = query_b.shape[-1]
    grad_soft = jnp.dot(grad_out, value_b.T, preferred_element_type=jnp.float32)
    grad_value = jnp.dot(
        soft_max.astype(jnp.bfloat16).T, grad_out, preferred_element_type=jnp.float32
    )
    grad_scores = soft_max * (grad_soft - jnp.sum(soft_max * grad_soft, axis=-1, keepdims=True))
    grad_scores_b = (grad_scores / math.sqrt(head_width)).astype(jnp.bfloat16)
    grad_query = jnp.dot(grad_scores_b, key_b, preferred_element_type=jnp.float32)
    grad_key = jnp.dot(grad_scores_b.T, query_b, preferred_element_type=jnp.float32)
    grad_q = rms_back(grad_query, q_unit, q_inverse, gains[0])
    grad_k = rms_back(grad_key, k_unit, k_inverse, gains[1])
    return jnp.concatenate([grad_q, grad_k, grad_value], axis=1).astype(jnp.bfloat16)


def guarded(active, func, operand):
    return lax.cond(active, func, lambda item: jax.tree.map(jnp.zeros_like, func(item)), operand)


def shards(
    clean, noise, timesteps, text_vec, w_embed, w_time, w_mod, w_qkv, w_out, qk_gain, w_final
):
    section = lax.axis_index("segment")
    batch_idx = lax.axis_index("dp")
    tok_rows = clean.shape[1]
    latent_width = clean.shape[2]
    model_width = w_embed.shape[2]
    seq_devices = lax.axis_size("seq")
    full_rows = tok_rows * seq_devices
    head_width = w_qkv.shape[4]
    head_total = w_qkv.shape[2] * seq_devices
    group_count = max(
        [
            count
            for count in range(1, seq_devices + 1)
            if seq_devices % count == 0 and count * tok_rows <= max(512, tok_rows)
        ]
    )
    block_rows = group_count * tok_rows
    block_total = full_rows // block_rows
    embed_w = w_embed[0]
    embed_f32 = embed_w.astype(jnp.float32)
    head_w = w_qkv[0, :, 0]
    flat_head_w = head_w.reshape(model_width, 3 * head_width)
    gains = qk_gain[0]
    final_w = w_final[0]
    step_pair = lax.dynamic_index_in_dim(timesteps, batch_idx, 0, keepdims=False)
    sigma_student = noise_level(step_pair[0])
    sigma_critic = noise_level(step_pair[1])
    own_step = jnp.where(section == 0, step_pair[0], step_pair[1])
    mod_piece = condition(own_step, text_vec[0], w_time[0], w_mod[0])
    modulation = lax.all_gather(mod_piece, "seq", axis=0, tiled=True)
    shift_in, scale_in, gate_vec, shift_out, scale_out = [
        modulation[slot * model_width : (slot + 1) * model_width] for slot in range(5)
    ]
    gathered_rows = lax.all_gather(w_out[0], "seq", axis=0, tiled=True)

    def input_rows(latent_block):
        embedded = jnp.dot(latent_block, embed_w, preferred_element_type=jnp.float32)
        normed, inverse = normalize(embedded)
        return (normed, inverse)

    def modulated_rows(latent_block):
        normed, _ = input_rows(latent_block)
        return (normed * (1.0 + scale_in) + shift_in).astype(jnp.bfloat16)

    def forward(latent_local, active):
        latent_all = lax.all_gather(latent_local, "seq", axis=0, tiled=True)

        def front(latent_rows):
            blocks = latent_rows.reshape(block_total, block_rows, latent_width)
            normed_in = lax.map(modulated_rows, blocks).reshape(full_rows, model_width)
            return head_front(normed_in, head_w, gains)

        head_out, stored = guarded(active, front, latent_all)
        own_rows = jnp.dot(latent_local, embed_w, preferred_element_type=jnp.float32)
        local_heads = lax.all_to_all(head_out, "seq", split_axis=0, concat_axis=1, tiled=True)

        def project(mixed):
            stacked = mixed.reshape(tok_rows, head_total, head_width)
            per_head = jnp.einsum(
                "thk,hkd->htd", stacked, gathered_rows, preferred_element_type=jnp.float32
            )
            return jnp.sum(
                lax.optimization_barrier(per_head.astype(jnp.bfloat16)).astype(jnp.float32), axis=0
            )

        attended = guarded(active, project, local_heads)
        residual = own_rows + gate_vec * attended
        normed_out, inverse_out = normalize(residual)
        final_in = (normed_out * (1.0 + scale_out) + shift_out).astype(jnp.bfloat16)
        result = jnp.dot(final_in, final_w, preferred_element_type=jnp.float32)
        return (result, final_in, (latent_all, stored, normed_out, inverse_out))

    noisy_student = (
        (1.0 - sigma_student) * clean[0].astype(jnp.float32)
        + sigma_student * noise[0, :, :latent_width].astype(jnp.float32)
    ).astype(jnp.bfloat16)
    velocity, student_in, _ = forward(noisy_student, section == 0)
    sample = noisy_student.astype(jnp.float32) - sigma_student * velocity
    sample = from_root(sample.astype(jnp.bfloat16), "segment", 0).astype(sample.dtype)
    second_noise = noise[0, :, latent_width:].astype(jnp.float32)
    noisy_critic = ((1.0 - sigma_critic) * sample + sigma_critic * second_noise).astype(
        jnp.bfloat16
    )
    critic_out, critic_in, cache = forward(noisy_critic, section >= 1)
    latent_all, stored, normed_out, inverse_out = cache
    is_judge = section == 3
    grad_logit = -jax.nn.sigmoid(-critic_out)
    grad_final = jnp.dot(
        grad_logit.astype(jnp.bfloat16), final_w.T, preferred_element_type=jnp.float32
    )
    grad_residual = normalize_back(grad_final * (1.0 + scale_out), normed_out, inverse_out)
    grad_attended = (gate_vec * grad_residual).astype(jnp.bfloat16)

    def spread_heads(grad_rows):
        per_head = jnp.einsum(
            "td,hkd->thk", grad_rows, gathered_rows, preferred_element_type=jnp.float32
        )
        return per_head.astype(jnp.bfloat16).reshape(tok_rows, head_total * head_width)

    grad_local = guarded(is_judge, spread_heads, grad_attended)
    grad_head = lax.all_to_all(grad_local, "seq", split_axis=1, concat_axis=0, tiled=True)
    grad_proj = guarded(is_judge, lambda grad_in: head_back(grad_in, stored, gains), grad_head)

    def latent_rows(first_row, row_count):

        def through(pieces):
            proj_rows, latent_block = pieces
            normed_rows, inverse_rows = input_rows(latent_block)
            grad_normed = jnp.dot(proj_rows, flat_head_w.T, preferred_element_type=jnp.float32)
            grad_embedded = normalize_back(
                grad_normed * (1.0 + scale_in), normed_rows, inverse_rows
            )
            return jnp.dot(grad_embedded, embed_f32.T, precision=lax.Precision.HIGHEST)

        pieces = tuple((source for source in (grad_proj, latent_all)))
        return guarded(is_judge, through, pieces)

    grad_latent = lax.psum_scatter(
        latent_rows(jnp.int32(0), tok_rows * lax.axis_size("seq")).astype(jnp.bfloat16),
        "seq",
        scatter_dimension=0,
        tiled=True,
    ).astype(jnp.float32)
    grad_latent = grad_latent + jnp.dot(grad_residual, embed_f32.T, precision=lax.Precision.HIGHEST)
    adverse = (1.0 - sigma_critic) * grad_latent
    real_part = jnp.where(section == 1, sigma_critic * critic_out, 0.0)
    fake_part = jnp.where(section == 2, sigma_critic * critic_out, 0.0)
    judge_part = jnp.where(is_judge, adverse, 0.0)
    real_term, fake_term, adverse_term = (
        lax.psum(real_part.astype(jnp.bfloat16), "segment").astype(jnp.float32),
        lax.psum(fake_part.astype(jnp.bfloat16), "segment").astype(jnp.float32),
        lax.psum(judge_part.astype(jnp.bfloat16), "segment").astype(jnp.float32),
    )
    error_local = jnp.sum(jnp.abs(sample - noisy_critic.astype(jnp.float32) + real_term))
    error_total = lax.psum(error_local, "seq")
    spread = error_total / (full_rows * latent_width) + EPS
    sample_grad = (real_term - fake_term) / spread + ADV_WEIGHT * adverse_term
    target = jnp.where(
        section == 0,
        -sigma_student * sample_grad,
        jnp.where(
            section == 2,
            2.0 * (critic_out - (second_noise - sample)),
            jnp.where(is_judge, jax.nn.sigmoid(critic_out), 0.0),
        ),
    )
    final_rows = jnp.where(section == 0, student_in, critic_in)
    term = jnp.einsum(
        "td,tc->dc", final_rows, target.astype(jnp.bfloat16), preferred_element_type=jnp.float32
    )
    total = lax.psum(term.astype(jnp.bfloat16), ("seq", "dp")).astype(jnp.float32)
    final_grads = total / full_rows
    return (sample_grad[None], final_grads[None])


def solution(mesh):
    placed = (
        P("dp", "seq", None),
        P("dp", "seq", None),
        P(),
        P("dp", None),
        P("segment", None, None),
        P("segment", None, None),
        P("segment", None, "seq"),
        P("segment", None, "seq", None, None),
        P("segment", "seq", None, None),
        P("segment", None, None),
        P("segment", None, None),
    )
    return jax.shard_map(
        shards,
        mesh=mesh,
        in_specs=placed,
        out_specs=(P("dp", "seq", None), P("segment", None, None)),
        check_vma=False,
    )
```

profile of v0, /device:TPU:0, one launch (start us, length us, event | category | flops | bytes accessed | tf_op | source)
XLA Modules:
  0.0 274.7 jit_solution(8759388569653749423)
XLA Ops:
  13.2 10.6 %fusion.34 = f32[1,1,3840]{2,1,0:T(1,128)S(1)} fusion(bf16[3072,1]{0,1:T(2,128)(2,1)S(1)} %reshape.223, bf16[1,3072,3840]{2,1,0:T(8,128)(2,1)} %param.31), kind=kOutput, calls=%fused_computation.97 | convolution fusion | flops 23592960 | bytes 23614464 | tf_op jit(solution)/shard_map/dot_general | solution.py:34
  23.8 6.7 %all-gather.2 = f32[4,1,3840]{2,1,0:T(1,128)S(1)} all-gather(f32[1,1,3840]{2,1,0:T(1,128)S(1)} %fusion.34), channel_id=1, replica_groups=mesh['segment'=4,'seq'=4,'dp'=2] {'seq'}, dimensions={0}, use_global_device_ids=true | all-gather | bytes 76800 | tf_op jit(solution)/shard_map/all_gather | solution.py:133
  30.4 6.0 %all-gather = bf16[1,512,64]{1,2,0:T(8,128)(2,1)S(1)} all-gather(bf16[1,128,64]{1,2,0:T(8,128)(2,1)S(1)} %add_convert_fusion.6), channel_id=2, replica_groups=mesh['segment'=4,'seq'=4,'dp'=2] {'seq'}, dimensions={1}, use_global_device_ids=true | all-gather | bytes 81920 | tf_op jit(solution)/shard_map/all_gather | solution.py:149
  37.1 9.9 %conditional.7 = (bf16[512,128]{1,0:T(8,128)(2,1)}) conditional(s32[]{:T(128)} %convert_element_type.187, () %tuple.57, (bf16[512,64]{0,1:T(8,128)(2,1)S(1)}, bf16[64,3072]{1,0:T(8,128)(2,1)S(1)}, f32[3072]{0:T(1024)}, f32[3072]{0:T(1024)}, bf16[1,3072,1,3,128]{4,1,3,2,0:T(8,128)(2,1)S(1)}, /*index=5*/f32[2,128]{1,0:T(2,128)S(1)}) %tuple.157), branch_computations={%region_0.1_spmd, %region_1.7_spmd} | conditional | flops 1559433216 | bytes 40133668 | solution.py:98
  37.8 2.4 copy.53
  43.0 2.4 fusion
  47.0 3.3 %all-to-all-start = ((bf16[4,128,128]{2,1,0:T(8,128)(2,1)}), bf16[4,128,128]{2,1,0:T(8,128)(2,1)S(1)}, u32[]{:S(2)}, u32[]{:S(2)}) async-start(bf16[4,128,128]{2,1,0:T(8,128)(2,1)} %bitcast.26), calls=%async_computation | async-start | bytes 262144 | tf_op jit(solution)/shard_map/all_to_all | solution.py:158
  51.0 3.9 %all-to-all-done = bf16[4,128,128]{2,1,0:T(8,128)(2,1)S(1)} async-done(((bf16[4,128,128]{2,1,0:T(8,128)(2,1)}), bf16[4,128,128]{2,1,0:T(8,128)(2,1)S(1)}, u32[]{:S(2)}, u32[]{:S(2)}) %all-to-all-start) | async-done | bytes 131104 | tf_op jit(solution)/shard_map/all_to_all | solution.py:158
  54.9 3.4 %conditional.8 = (f32[128,3072]{1,0:T(8,128)S(1)}) conditional(s32[]{:T(128)} %convert_element_type.187, () %tuple.56, (bf16[128,4,128]{2,0,1:T(8,128)(2,1)S(1)}, bf16[4,128,3072]{2,1,0:T(8,128)(2,1)}) %tuple.152), branch_computations={%region_7.8_spmd, %region_8.10_spmd} | conditional | flops 406978560 | bytes 11141128 | solution.py:98
  54.9 2.9 %convolution_convert_fusion.1 = bf16[4,128,3072]{2,1,0:T(8,128)(2,1)S(1)} fusion(bf16[128,4,128]{2,0,1:T(8,128)(2,1)S(1)} %get-tuple-element.132, bf16[4,128,3072]{2,1,0:T(8,128)(2,1)} %get-tuple-element.133), kind=kOutput, calls=%fused_computation.28 | convolution fusion | flops 404226048 | bytes 6422528 | tf_op jit(solution)/shard_map/cond/branch_1_fun/thk,hkd->htd/dot_general | solution.py:162
  60.8 15.5 %psum.42 = bf16[128,64]{0,1:T(8,128)(2,1)S(1)} all-reduce(bf16[128,64]{0,1:T(8,128)(2,1)S(1)} %fusion.44), channel_id=1, replica_groups=mesh['segment'=4,'seq'=4,'dp'=2] {'segment'}, use_global_device_ids=true, to_apply=%region_12.13 | all-reduce | flops 8192 | bytes 32768 | tf_op jit(solution)/shard_map/psum | solution.py:14
  76.4 5.7 %all_gather.15 = bf16[512,64]{0,1:T(8,128)(2,1)} all-gather(bf16[128,64]{0,1:T(8,128)(2,1)S(1)} %fusion.56), channel_id=1, replica_groups=mesh['segment'=4,'seq'=4,'dp'=2] {'seq'}, dimensions={0}, use_global_device_ids=true | all-gather | bytes 81920 | tf_op jit(solution)/shard_map/all_gather | solution.py:149
  82.1 5.8 %conditional.9 = (bf16[512,128]{1,0:T(8,128)(2,1)S(1)}, f32[512,128]{0,1:T(8,128)}, f32[512,1]{0,1:T(1,128)}, f32[512,128]{0,1:T(8,128)}, f32[512,1]{0,1:T(1,128...) conditional(s32[]{:T(128)} %convert_element_type.194, () %tuple.61, ...), branch_computations={%region_13.14_spmd, %region_14.20_spmd} | conditional | flops 1559433216 | bytes 43594936 | solution.py:98
  88.5 3.9 %all-to-all-start.1 = ((bf16[4,128,128]{2,1,0:T(8,128)(2,1)}), bf16[4,128,128]{2,1,0:T(8,128)(2,1)}, u32[]{:S(2)}, u32[]{:S(2)}) async-start(bf16[4,128,128]{2,1,0:T(8,128)(2,1)} %bitcast.134), calls=%async_computation.1 | async-start | bytes 262144 | tf_op jit(solution)/shard_map/all_to_all | solution.py:158
  92.5 4.7 %all-to-all-done.1 = bf16[4,128,128]{2,1,0:T(8,128)(2,1)} async-done(((bf16[4,128,128]{2,1,0:T(8,128)(2,1)}), bf16[4,128,128]{2,1,0:T(8,128)(2,1)}, u32[]{:S(2)}, u32[]{:S(2)}) %all-to-all-start.1) | async-done | bytes 131104 | tf_op jit(solution)/shard_map/all_to_all | solution.py:158
  102.0 2.1 select_convert_fusion
  104.8 2.0 multiply_convert_fusion.9
  107.5 3.3 %all-to-all-start.2 = ((bf16[128,4,128]{0,2,1:T(8,128)(2,1)}), bf16[128,4,128]{0,2,1:T(8,128)(2,1)S(1)}, u32[]{:S(2)}, u32[]{:S(2)}) async-start(bf16[128,4,128]{0,2,1:T(8,128)(2,1)} %bitcast.33), calls=%async_computation.2 | async-start | bytes 262144 | tf_op jit(solution)/shard_map/all_to_all | solution.py:204
  110.9 4.5 %all-to-all-done.2 = bf16[128,4,128]{0,2,1:T(8,128)(2,1)S(1)} async-done(((bf16[128,4,128]{0,2,1:T(8,128)(2,1)}), bf16[128,4,128]{0,2,1:T(8,128)(2,1)S(1)}, u32[]{:S(2)}, u32[]{:S(2)}) %all-to-all-start.2) | async-done | bytes 131104 | tf_op jit(solution)/shard_map/all_to_all | solution.py:204
  119.6 60.8 %reduce-scatter.4.cloned.1.call-done = bf16[128,64]{1,0:T(8,128)(2,1)} async-done(((bf16[512,64]{1,0:T(8,128)(2,1)}), bf16[128,64]{1,0:T(8,128)(2,1)}) %reduce-scatter.4.cloned.1.call-update) | async-done | bytes 16400
  181.2 2.5 fusion.43
  183.7 19.9 %all-reduce = (bf16[128,64]{0,1:T(8,128)(2,1)S(1)}, bf16[128,64]{0,1:T(8,128)(2,1)S(1)}, bf16[128,64]{0,1:T(8,128)(2,1)S(1)}) all-reduce(bf16[128,64]{0,1:T(8,128)(2,1)S(1)} %fusion.43, bf16[128,64]{0,1:T(8,128)(2,1)} %get-tuple-element.343, ...), channel_id=1, replica_groups=mesh['segment'=4,'seq'=4,'dp'=2] {'segment'}, use_global_device_ids=true, to_apply=%region_45.46 | all-reduce | flops 24576 | bytes 98304 | tf_op jit(solution)/shard_map/psum | solution.py:235
  205.0 6.6 %psum.45 = f32[]{:T(128)} all-reduce(f32[]{:T(128)} %fusion.54), channel_id=1, replica_groups=mesh['segment'=4,'seq'=4,'dp'=2] {'seq'}, use_global_device_ids=true, to_apply=%region_28.29 | all-reduce | flops 1 | bytes 8 | tf_op jit(solution)/shard_map/psum | solution.py:238
  214.6 51.6 %all-reduce.3.cloned.1.call-done = bf16[3072,64]{0,1:T(8,128)(2,1)} async-done(((bf16[3072,64]{0,1:T(8,128)(2,1)}), bf16[3072,64]{0,1:T(8,128)(2,1)}) %all-reduce.3.cloned.1.call-update) | async-done | bytes 393232 | tf_op jit(solution)/shard_map/psum | solution.py:254
  (115 shorter events, 38.8 us)
Async XLA Ops:
  7.2 3.9 %copy-start = (bf16[1,256,3072]{2,1,0:T(8,128)(2,1)S(1)}, bf16[1,256,3072]{2,1,0:T(8,128)(2,1)}, u32[]{:S(2)}) copy-start(bf16[1,256,3072]{2,1,0:T(8,128)(2,1)} %param.30) | copy-start | bytes 4718596
  7.2 47.7 %all-gather.5.cloned.1.call-start = ((), (), s32[]{:S(2)}) async-start(), calls=%async_computation.5 | async-start | bytes 3932160 | tf_op jit(solution)/shard_map/all_gather | solution.py:137
  13.2 17.3 %copy-start.26 = (bf16[1,128,64]{1,2,0:T(8,128)(2,1)S(1)}, bf16[1,128,64]{1,2,0:T(8,128)(2,1)}, u32[]{:S(2)}) copy-start(bf16[1,128,64]{1,2,0:T(8,128)(2,1)} %param.25) | copy-start | bytes 49156
  13.2 23.9 %copy-start.3 = (bf16[1,3072,1,3,128]{4,1,3,2,0:T(8,128)(2,1)S(1)}, bf16[1,3072,1,3,128]{4,1,3,2,0:T(8,128)(2,1)}, u32[]{:S(2)}) copy-start(bf16[1,3072,1,3,128]{4,1,3,2,0:T(8,128)(2,1)} %param.32) | copy-start | bytes 7077892
  13.2 23.9 %copy-start.5 = (bf16[1,64,3072]{2,1,0:T(8,128)(2,1)S(1)}, bf16[1,64,3072]{2,1,0:T(8,128)(2,1)}, u32[]{:S(2)}) copy-start(bf16[1,64,3072]{2,1,0:T(8,128)(2,1)} %param.29) | copy-start | bytes 1179652
  13.2 23.9 %copy-start.28 = (f32[1,2,128]{2,1,0:T(2,128)S(1)}, f32[1,2,128]{2,1,0:T(2,128)}, u32[]{:S(2)}) copy-start(f32[1,2,128]{2,1,0:T(2,128)} %param.34) | copy-start | bytes 3076
  37.0 21.3 %copy-start.18 = (f32[3072]{0:T(1024)}, f32[3072]{0:T(1024)S(1)}, u32[]{:S(2)}) copy-start(f32[3072]{0:T(1024)S(1)} %get-tuple-element.341) | copy-start | bytes 36868
  37.0 22.1 %copy-start.20 = (f32[3072]{0:T(1024)}, f32[3072]{0:T(1024)S(1)}, u32[]{:S(2)}) copy-start(f32[3072]{0:T(1024)S(1)} %get-tuple-element.338) | copy-start | bytes 36868
  37.0 22.1 %copy-start.24 = (f32[3072]{0:T(1024)}, f32[3072]{0:T(1024)S(1)}, u32[]{:S(2)}) copy-start(f32[3072]{0:T(1024)S(1)} %get-tuple-element.337) | copy-start | bytes 36868
  47.0 7.9 %all-to-all-start = ((bf16[4,128,128]{2,1,0:T(8,128)(2,1)}), bf16[4,128,128]{2,1,0:T(8,128)(2,1)S(1)}, u32[]{:S(2)}, u32[]{:S(2)}) async-start(bf16[4,128,128]{2,1,0:T(8,128)(2,1)} %bitcast.26), calls=%async_computation | async-start | bytes 262144 | tf_op jit(solution)/shard_map/all_to_all | solution.py:158
  51.0 25.4 %copy-start.23 = (bf16[1,128,64]{1,2,0:T(8,128)(2,1)}, bf16[1,128,64]{1,2,0:T(8,128)(2,1)S(1)}, u32[]{:S(2)}) copy-start(bf16[1,128,64]{1,2,0:T(8,128)(2,1)S(1)} %copy.74) | copy-start | bytes 49156
  58.3 2.1 copy-start.9
  76.4 5.7 %copy-start.17 = (bf16[128,64]{0,1:T(8,128)(2,1)}, bf16[128,64]{0,1:T(8,128)(2,1)S(1)}, u32[]{:S(2)}) copy-start(bf16[128,64]{0,1:T(8,128)(2,1)S(1)} %psum.42) | copy-start | bytes 49156
  82.1 15.0 %copy-start.2 = (bf16[4,1,128,3072]{3,2,1,0:T(8,128)(2,1)S(1)}, bf16[4,1,128,3072]{3,2,1,0:T(8,128)(2,1)}, u32[]{:S(2)}) copy-start(bf16[4,1,128,3072]{3,2,1,0:T(8,128)(2,1)} %all-gather.5.cloned.1.call-done) | copy-start | bytes 9437188
  88.5 8.6 %all-to-all-start.1 = ((bf16[4,128,128]{2,1,0:T(8,128)(2,1)}), bf16[4,128,128]{2,1,0:T(8,128)(2,1)}, u32[]{:S(2)}, u32[]{:S(2)}) async-start(bf16[4,128,128]{2,1,0:T(8,128)(2,1)} %bitcast.134), calls=%async_computation.1 | async-start | bytes 262144 | tf_op jit(solution)/shard_map/all_to_all | solution.py:158
  98.5 2.3 copy-start.21
  98.5 2.3 copy-start.25
  98.5 3.5 %copy-start.10 = (bf16[1,3072,64]{1,2,0:T(8,128)(2,1)S(1)}, bf16[1,3072,64]{1,2,0:T(8,128)(2,1)}, u32[]{:S(2)}) copy-start(bf16[1,3072,64]{1,2,0:T(8,128)(2,1)} %param.35) | copy-start | bytes 1179652
  100.8 4.0 %copy-start.19 = (f32[3072]{0:T(1024)S(1)}, f32[3072]{0:T(1024)}, u32[]{:S(2)}) copy-start(f32[3072]{0:T(1024)} %copy-done.18) | copy-start | bytes 36868
  107.5 7.9 %all-to-all-start.2 = ((bf16[128,4,128]{0,2,1:T(8,128)(2,1)}), bf16[128,4,128]{0,2,1:T(8,128)(2,1)S(1)}, u32[]{:S(2)}, u32[]{:S(2)}) async-start(bf16[128,4,128]{0,2,1:T(8,128)(2,1)} %bitcast.33), calls=%async_computation.2 | async-start | bytes 262144 | tf_op jit(solution)/shard_map/all_to_all | solution.py:204
  110.8 69.6 %reduce-scatter.4.cloned.1.call-start = ((), (), s32[]{:S(2)}) async-start(), calls=%async_computation.6 | async-start | bytes 163840
  117.2 94.9 %copy-start.8 = (bf16[128,3072]{1,0:T(8,128)(2,1)S(1)}, bf16[128,3072]{1,0:T(8,128)(2,1)}, u32[]{:S(2)}) copy-start(bf16[128,3072]{1,0:T(8,128)(2,1)} %copy-done.7) | copy-start | bytes 2359300
  117.8 150.3 %copy-start.1 = (bf16[1,256,3072]{2,1,0:T(8,128)(2,1)S(1)}, bf16[1,256,3072]{2,1,0:T(8,128)(2,1)}, u32[]{:S(2)}) copy-start(bf16[1,256,3072]{2,1,0:T(8,128)(2,1)} %param.30) | copy-start | bytes 4718596
  119.6 146.6 %all-reduce.3.cloned.1.call-start = ((), (), s32[]{:S(2)}) async-start(), calls=%async_computation.4 | async-start | bytes 786432 | tf_op jit(solution)/shard_map/psum | solution.py:254
  (6 other events, 6.5 us)
Sparse Core Ops, SparseCore 0:
  9.5 31.9 all-gather.4
  119.7 60.6 reduce-scatter.3
  214.1 52.0 all-reduce.2
where the time goes:
time: 276 us; the launch traced here: 275 us
  waiting for transfers between devices  126 us (46%)
  blocking collectives  60.4 us (22%)
  matrix products  29.3 us (11%)
  local copies, waits for them, and re-layouts  20 us (7%)
  between operations  17.2 us (6%)
  other arithmetic  10.9 us (4%)
  starting transfers between devices  10.7 us (4%)
    unnamed x4, waiting for transfers between devices  61.5 us
    psum x1, waiting for transfers between devices, shards(): lax.psum(term.astype(jnp.bfloat16), ('seq', 'dp')).astype(jnp.float32)  51.6 us
    psum x1, blocking collectives, shards(): lax.psum(judge_part.astype(jnp.bfloat16), 'segment').astype(jnp.float32)  19.9 us
    psum x1, blocking collectives, from_root(): return lax.psum(kept, axis)  15.5 us
    all_gather x2, blocking collectives, forward(): latent_all = lax.all_gather(latent_local, 'seq', axis=0, tiled=True)  11.7 us
    another operation x14, local copies, waits for them, and re-layouts  10.8 us
    dot_general x1, matrix products, condition(): return jnp.dot(hidden, mod_w, preferred_element_type=jnp.float32)  10.6 us
    all_to_all x2, waiting for transfers between devices, forward(): lax.all_to_all(head_out, 'seq', split_axis=0, concat_axis=1, tiled=True)  8.52 us
  transfers between devices with their start and end apart: 6, of which 5 were waited for; matrix products, arithmetic and copies ran while one was open for 9% of the time, Pallas kernels for 0%

commit v1 on v0

--- a/solution.py
+++ b/solution.py
@@ -232,7 +232,9 @@
     real_term, fake_term, adverse_term = (
         lax.psum(real_part.astype(jnp.bfloat16), "segment").astype(jnp.float32),
         lax.psum(fake_part.astype(jnp.bfloat16), "segment").astype(jnp.float32),
-        lax.psum(judge_part.astype(jnp.bfloat16), "segment").astype(jnp.float32),
+        jnp.sum(lax.all_gather(judge_part.astype(jnp.bfloat16), "segment"), axis=0).astype(
+            jnp.float32
+        ),
     )
     error_local = jnp.sum(jnp.abs(sample - noisy_critic.astype(jnp.float32) + real_term))
     error_total = lax.psum(error_local, "seq")

time: 276 us -> 267 us (0.967)
  waiting for transfers between devices: 126 us -> 65.8 us
  blocking collectives: 60.4 us -> 113 us
    unnamed x4, waiting for transfers between devices: 61.5 us -> 0.73 us
    psum x1, blocking collectives: 19.9 us -> 60.4 us  [shards(): lax.psum(real_part.astype(jnp.bfloat16), 'segment').astype(jnp.float32)]
    all_gather x0 -> x1, blocking collectives: none -> 12 us  [shards(): lax.all_gather(judge_part.astype(jnp.bfloat16), 'segment')]
  transfers between devices with their start and end apart: 6 -> 6, of which waited for: 5 -> 4; matrix products, arithmetic and copies ran while one was open for 9% -> 10% of each run, Pallas kernels for 0% -> 0%
where the time goes in v1:
time: 267 us; the launch traced here: 265 us
  blocking collectives  113 us (42%)
  waiting for transfers between devices  65.8 us (25%)
  matrix products  29.3 us (11%)
  local copies, waits for them, and re-layouts  18.5 us (7%)
  between operations  17.2 us (6%)
  other arithmetic  11 us (4%)
  starting transfers between devices  10.7 us (4%)
    psum x1, blocking collectives, shards(): lax.psum(real_part.astype(jnp.bfloat16), 'segment').astype(jnp.float32)  60.4 us
    psum x1, waiting for transfers between devices, shards(): lax.psum(term.astype(jnp.bfloat16), ('seq', 'dp')).astype(jnp.float32)  52 us
    psum x1, blocking collectives, from_root(): return lax.psum(kept, axis)  15.5 us
    all_gather x1, blocking collectives, shards(): lax.all_gather(judge_part.astype(jnp.bfloat16), 'segment')  12 us
    all_gather x2, blocking collectives, forward(): latent_all = lax.all_gather(latent_local, 'seq', axis=0, tiled=True)  11.7 us
    dot_general x1, matrix products, condition(): return jnp.dot(hidden, mod_w, preferred_element_type=jnp.float32)  10.6 us
    another operation x14, local copies, waits for them, and re-layouts  10.2 us
    all_to_all x2, waiting for transfers between devices, forward(): lax.all_to_all(head_out, 'seq', split_axis=0, concat_axis=1, tiled=True)  8.52 us
  transfers between devices with their start and end apart: 6, of which 4 were waited for; matrix products, arithmetic and copies ran while one was open for 10% of the time, Pallas kernels for 0%

profile of v1, /device:TPU:0, one launch (start us, length us, event | category | flops | bytes accessed | tf_op | source)
XLA Modules:
  0.0 265.5 jit_solution(8640600513980821520)
XLA Ops:
  13.2 10.6 %fusion.34 = f32[1,1,3840]{2,1,0:T(1,128)S(1)} fusion(bf16[3072,1]{0,1:T(2,128)(2,1)S(1)} %reshape.224, bf16[1,3072,3840]{2,1,0:T(8,128)(2,1)} %param.31), kind=kOutput, calls=%fused_computation.97 | convolution fusion | flops 23592960 | bytes 23614464 | tf_op jit(solution)/shard_map/dot_general | solution.py:34
  23.8 6.7 %all-gather.3 = f32[4,1,3840]{2,1,0:T(1,128)S(1)} all-gather(f32[1,1,3840]{2,1,0:T(1,128)S(1)} %fusion.34), channel_id=1, replica_groups=mesh['segment'=4,'seq'=4,'dp'=2] {'seq'}, dimensions={0}, use_global_device_ids=true | all-gather | bytes 76800 | tf_op jit(solution)/shard_map/all_gather | solution.py:133
  30.4 6.0 %all-gather = bf16[1,512,64]{1,2,0:T(8,128)(2,1)S(1)} all-gather(bf16[1,128,64]{1,2,0:T(8,128)(2,1)S(1)} %add_convert_fusion.6), channel_id=2, replica_groups=mesh['segment'=4,'seq'=4,'dp'=2] {'seq'}, dimensions={1}, use_global_device_ids=true | all-gather | bytes 81920 | tf_op jit(solution)/shard_map/all_gather | solution.py:149
  37.1 9.9 %conditional.7 = (bf16[512,128]{1,0:T(8,128)(2,1)}) conditional(s32[]{:T(128)} %convert_element_type.189, () %tuple.57, (bf16[512,64]{0,1:T(8,128)(2,1)S(1)}, bf16[64,3072]{1,0:T(8,128)(2,1)S(1)}, f32[3072]{0:T(1024)}, f32[3072]{0:T(1024)}, bf16[1,3072,1,3,128]{4,1,3,2,0:T(8,128)(2,1)S(1)}, /*index=5*/f32[2,128]{1,0:T(2,128)S(1)}) %tuple.157), branch_computations={%region_0.1_spmd, %region_1.7_spmd} | conditional | flops 1559433216 | bytes 40133668 | solution.py:98
  37.8 2.4 copy.53
  43.0 2.4 fusion
  47.0 3.3 %all-to-all-start = ((bf16[4,128,128]{2,1,0:T(8,128)(2,1)}), bf16[4,128,128]{2,1,0:T(8,128)(2,1)S(1)}, u32[]{:S(2)}, u32[]{:S(2)}) async-start(bf16[4,128,128]{2,1,0:T(8,128)(2,1)} %bitcast.26), calls=%async_computation | async-start | bytes 262144 | tf_op jit(solution)/shard_map/all_to_all | solution.py:158
  51.0 3.9 %all-to-all-done = bf16[4,128,128]{2,1,0:T(8,128)(2,1)S(1)} async-done(((bf16[4,128,128]{2,1,0:T(8,128)(2,1)}), bf16[4,128,128]{2,1,0:T(8,128)(2,1)S(1)}, u32[]{:S(2)}, u32[]{:S(2)}) %all-to-all-start) | async-done | bytes 131104 | tf_op jit(solution)/shard_map/all_to_all | solution.py:158
  54.9 3.4 %conditional.8 = (f32[128,3072]{1,0:T(8,128)S(1)}) conditional(s32[]{:T(128)} %convert_element_type.189, () %tuple.56, (bf16[128,4,128]{2,0,1:T(8,128)(2,1)S(1)}, bf16[4,128,3072]{2,1,0:T(8,128)(2,1)}) %tuple.152), branch_computations={%region_7.8_spmd, %region_8.10_spmd} | conditional | flops 406978560 | bytes 11141128 | solution.py:98
  54.9 2.9 %convolution_convert_fusion.1 = bf16[4,128,3072]{2,1,0:T(8,128)(2,1)S(1)} fusion(bf16[128,4,128]{2,0,1:T(8,128)(2,1)S(1)} %get-tuple-element.132, bf16[4,128,3072]{2,1,0:T(8,128)(2,1)} %get-tuple-element.133), kind=kOutput, calls=%fused_computation.28 | convolution fusion | flops 404226048 | bytes 6422528 | tf_op jit(solution)/shard_map/cond/branch_1_fun/thk,hkd->htd/dot_general | solution.py:162
  60.8 15.5 %psum.35 = bf16[128,64]{0,1:T(8,128)(2,1)S(1)} all-reduce(bf16[128,64]{0,1:T(8,128)(2,1)S(1)} %fusion.44), channel_id=1, replica_groups=mesh['segment'=4,'seq'=4,'dp'=2] {'segment'}, use_global_device_ids=true, to_apply=%region_12.13 | all-reduce | flops 8192 | bytes 32768 | tf_op jit(solution)/shard_map/psum | solution.py:14
  76.4 5.7 %all_gather.21 = bf16[512,64]{0,1:T(8,128)(2,1)} all-gather(bf16[128,64]{0,1:T(8,128)(2,1)S(1)} %fusion.56), channel_id=1, replica_groups=mesh['segment'=4,'seq'=4,'dp'=2] {'seq'}, dimensions={0}, use_global_device_ids=true | all-gather | bytes 81920 | tf_op jit(solution)/shard_map/all_gather | solution.py:149
  82.1 5.8 %conditional.9 = (bf16[512,128]{1,0:T(8,128)(2,1)S(1)}, f32[512,128]{0,1:T(8,128)}, f32[512,1]{0,1:T(1,128)}, f32[512,128]{0,1:T(8,128)}, f32[512,1]{0,1:T(1,128...) conditional(s32[]{:T(128)} %convert_element_type.196, () %tuple.61, ...), branch_computations={%region_13.14_spmd, %region_14.20_spmd} | conditional | flops 1559433216 | bytes 43594936 | solution.py:98
  88.5 3.9 %all-to-all-start.1 = ((bf16[4,128,128]{2,1,0:T(8,128)(2,1)}), bf16[4,128,128]{2,1,0:T(8,128)(2,1)}, u32[]{:S(2)}, u32[]{:S(2)}) async-start(bf16[4,128,128]{2,1,0:T(8,128)(2,1)} %bitcast.136), calls=%async_computation.1 | async-start | bytes 262144 | tf_op jit(solution)/shard_map/all_to_all | solution.py:158
  92.5 4.7 %all-to-all-done.1 = bf16[4,128,128]{2,1,0:T(8,128)(2,1)} async-done(((bf16[4,128,128]{2,1,0:T(8,128)(2,1)}), bf16[4,128,128]{2,1,0:T(8,128)(2,1)}, u32[]{:S(2)}, u32[]{:S(2)}) %all-to-all-start.1) | async-done | bytes 131104 | tf_op jit(solution)/shard_map/all_to_all | solution.py:158
  102.0 2.1 select_convert_fusion
  104.8 2.0 multiply_convert_fusion.9
  107.5 3.3 %all-to-all-start.2 = ((bf16[128,4,128]{0,2,1:T(8,128)(2,1)}), bf16[128,4,128]{0,2,1:T(8,128)(2,1)S(1)}, u32[]{:S(2)}, u32[]{:S(2)}) async-start(bf16[128,4,128]{0,2,1:T(8,128)(2,1)} %bitcast.33), calls=%async_computation.2 | async-start | bytes 262144 | tf_op jit(solution)/shard_map/all_to_all | solution.py:204
  110.9 4.5 %all-to-all-done.2 = bf16[128,4,128]{0,2,1:T(8,128)(2,1)S(1)} async-done(((bf16[128,4,128]{0,2,1:T(8,128)(2,1)}), bf16[128,4,128]{0,2,1:T(8,128)(2,1)S(1)}, u32[]{:S(2)}, u32[]{:S(2)}) %all-to-all-start.2) | async-done | bytes 131104 | tf_op jit(solution)/shard_map/all_to_all | solution.py:204
  118.3 60.4 %all-reduce = (bf16[128,64]{0,1:T(8,128)(2,1)S(1)}, bf16[128,64]{0,1:T(8,128)(2,1)S(1)}) all-reduce(bf16[128,64]{0,1:T(8,128)(2,1)} %get-tuple-element.342, bf16[128,64]{0,1:T(8,128)(2,1)} %get-tuple-element.341), channel_id=1, replica_groups=mesh['segment'=4,'seq'=4,'dp'=2] {'segment'}, use_global_device_ids=true, to_apply=%region_25.26 | all-reduce | flops 16384 | bytes 65536 | tf_op jit(solution)/shard_map/psum | solution.py:233
  180.0 6.5 %psum.38 = f32[]{:T(128)} all-reduce(f32[]{:T(128)} %fusion.54), channel_id=1, replica_groups=mesh['segment'=4,'seq'=4,'dp'=2] {'seq'}, use_global_device_ids=true, to_apply=%region_28.29 | all-reduce | flops 1 | bytes 8 | tf_op jit(solution)/shard_map/psum | solution.py:240
  187.9 2.5 fusion.43
  190.3 12.0 %all-gather.2 = bf16[512,64]{0,1:T(8,128)(2,1)S(1)} all-gather(bf16[128,64]{0,1:T(8,128)(2,1)S(1)} %fusion.43), channel_id=4, replica_groups=mesh['segment'=4,'seq'=4,'dp'=2] {'segment'}, dimensions={0}, use_global_device_ids=true | all-gather | bytes 81920 | tf_op jit(solution)/shard_map/all_gather | solution.py:235
  205.0 52.0 %all-reduce.3.cloned.1.call-done = bf16[3072,64]{0,1:T(8,128)(2,1)} async-done(((bf16[3072,64]{0,1:T(8,128)(2,1)}), bf16[3072,64]{0,1:T(8,128)(2,1)}) %all-reduce.3.cloned.1.call-update) | async-done | bytes 393232 | tf_op jit(solution)/shard_map/psum | solution.py:256
  (118 shorter events, 37.0 us)
Async XLA Ops:
  7.2 3.9 %copy-start = (bf16[1,256,3072]{2,1,0:T(8,128)(2,1)S(1)}, bf16[1,256,3072]{2,1,0:T(8,128)(2,1)}, u32[]{:S(2)}) copy-start(bf16[1,256,3072]{2,1,0:T(8,128)(2,1)} %param.30) | copy-start | bytes 4718596
  7.2 47.7 %all-gather.6.cloned.1.call-start = ((), (), s32[]{:S(2)}) async-start(), calls=%async_computation.5 | async-start | bytes 3932160 | tf_op jit(solution)/shard_map/all_gather | solution.py:137
  13.2 17.3 %copy-start.26 = (bf16[1,128,64]{1,2,0:T(8,128)(2,1)S(1)}, bf16[1,128,64]{1,2,0:T(8,128)(2,1)}, u32[]{:S(2)}) copy-start(bf16[1,128,64]{1,2,0:T(8,128)(2,1)} %param.25) | copy-start | bytes 49156
  13.2 23.9 %copy-start.3 = (bf16[1,3072,1,3,128]{4,1,3,2,0:T(8,128)(2,1)S(1)}, bf16[1,3072,1,3,128]{4,1,3,2,0:T(8,128)(2,1)}, u32[]{:S(2)}) copy-start(bf16[1,3072,1,3,128]{4,1,3,2,0:T(8,128)(2,1)} %param.32) | copy-start | bytes 7077892
  13.2 23.9 %copy-start.5 = (bf16[1,64,3072]{2,1,0:T(8,128)(2,1)S(1)}, bf16[1,64,3072]{2,1,0:T(8,128)(2,1)}, u32[]{:S(2)}) copy-start(bf16[1,64,3072]{2,1,0:T(8,128)(2,1)} %param.29) | copy-start | bytes 1179652
  13.2 23.9 %copy-start.28 = (f32[1,2,128]{2,1,0:T(2,128)S(1)}, f32[1,2,128]{2,1,0:T(2,128)}, u32[]{:S(2)}) copy-start(f32[1,2,128]{2,1,0:T(2,128)} %param.34) | copy-start | bytes 3076
  37.0 21.3 %copy-start.18 = (f32[3072]{0:T(1024)}, f32[3072]{0:T(1024)S(1)}, u32[]{:S(2)}) copy-start(f32[3072]{0:T(1024)S(1)} %get-tuple-element.340) | copy-start | bytes 36868
  37.0 22.1 %copy-start.20 = (f32[3072]{0:T(1024)}, f32[3072]{0:T(1024)S(1)}, u32[]{:S(2)}) copy-start(f32[3072]{0:T(1024)S(1)} %get-tuple-element.337) | copy-start | bytes 36868
  37.0 22.1 %copy-start.24 = (f32[3072]{0:T(1024)}, f32[3072]{0:T(1024)S(1)}, u32[]{:S(2)}) copy-start(f32[3072]{0:T(1024)S(1)} %get-tuple-element.336) | copy-start | bytes 36868
  47.0 7.9 %all-to-all-start = ((bf16[4,128,128]{2,1,0:T(8,128)(2,1)}), bf16[4,128,128]{2,1,0:T(8,128)(2,1)S(1)}, u32[]{:S(2)}, u32[]{:S(2)}) async-start(bf16[4,128,128]{2,1,0:T(8,128)(2,1)} %bitcast.26), calls=%async_computation | async-start | bytes 262144 | tf_op jit(solution)/shard_map/all_to_all | solution.py:158
  51.0 25.4 %copy-start.23 = (bf16[1,128,64]{1,2,0:T(8,128)(2,1)}, bf16[1,128,64]{1,2,0:T(8,128)(2,1)S(1)}, u32[]{:S(2)}) copy-start(bf16[1,128,64]{1,2,0:T(8,128)(2,1)S(1)} %copy.74) | copy-start | bytes 49156
  58.3 2.1 copy-start.9
  76.4 5.7 %copy-start.17 = (bf16[128,64]{0,1:T(8,128)(2,1)}, bf16[128,64]{0,1:T(8,128)(2,1)S(1)}, u32[]{:S(2)}) copy-start(bf16[128,64]{0,1:T(8,128)(2,1)S(1)} %psum.35) | copy-start | bytes 49156
  82.1 15.0 %copy-start.2 = (bf16[4,1,128,3072]{3,2,1,0:T(8,128)(2,1)S(1)}, bf16[4,1,128,3072]{3,2,1,0:T(8,128)(2,1)}, u32[]{:S(2)}) copy-start(bf16[4,1,128,3072]{3,2,1,0:T(8,128)(2,1)} %all-gather.6.cloned.1.call-done) | copy-start | bytes 9437188
  88.5 8.6 %all-to-all-start.1 = ((bf16[4,128,128]{2,1,0:T(8,128)(2,1)}), bf16[4,128,128]{2,1,0:T(8,128)(2,1)}, u32[]{:S(2)}, u32[]{:S(2)}) async-start(bf16[4,128,128]{2,1,0:T(8,128)(2,1)} %bitcast.136), calls=%async_computation.1 | async-start | bytes 262144 | tf_op jit(solution)/shard_map/all_to_all | solution.py:158
  98.5 2.3 copy-start.21
  98.5 2.3 copy-start.25
  98.5 3.5 %copy-start.10 = (bf16[1,3072,64]{1,2,0:T(8,128)(2,1)S(1)}, bf16[1,3072,64]{1,2,0:T(8,128)(2,1)}, u32[]{:S(2)}) copy-start(bf16[1,3072,64]{1,2,0:T(8,128)(2,1)} %param.35) | copy-start | bytes 1179652
  100.8 4.0 %copy-start.19 = (f32[3072]{0:T(1024)S(1)}, f32[3072]{0:T(1024)}, u32[]{:S(2)}) copy-start(f32[3072]{0:T(1024)} %copy-done.18) | copy-start | bytes 36868
  107.5 7.9 %all-to-all-start.2 = ((bf16[128,4,128]{0,2,1:T(8,128)(2,1)}), bf16[128,4,128]{0,2,1:T(8,128)(2,1)S(1)}, u32[]{:S(2)}, u32[]{:S(2)}) async-start(bf16[128,4,128]{0,2,1:T(8,128)(2,1)} %bitcast.33), calls=%async_computation.2 | async-start | bytes 262144 | tf_op jit(solution)/shard_map/all_to_all | solution.py:204
  110.8 76.2 %reduce-scatter.4.cloned.1.call-start = ((), (), s32[]{:S(2)}) async-start(), calls=%async_computation.6 | async-start | bytes 163840
  117.2 85.3 %copy-start.8 = (bf16[128,3072]{1,0:T(8,128)(2,1)S(1)}, bf16[128,3072]{1,0:T(8,128)(2,1)}, u32[]{:S(2)}) copy-start(bf16[128,3072]{1,0:T(8,128)(2,1)} %copy-done.7) | copy-start | bytes 2359300
  118.2 140.8 %copy-start.1 = (bf16[1,256,3072]{2,1,0:T(8,128)(2,1)S(1)}, bf16[1,256,3072]{2,1,0:T(8,128)(2,1)}, u32[]{:S(2)}) copy-start(bf16[1,256,3072]{2,1,0:T(8,128)(2,1)} %param.30) | copy-start | bytes 4718596
  118.2 138.8 %all-reduce.3.cloned.1.call-start = ((), (), s32[]{:S(2)}) async-start(), calls=%async_computation.4 | async-start | bytes 786432 | tf_op jit(solution)/shard_map/psum | solution.py:256
  (6 other events, 6.5 us)
Sparse Core Ops, SparseCore 0:
  9.5 31.9 all-gather.5
  118.3 60.4 reduce-scatter.3
  204.5 52.5 all-reduce.2
